TPU v7x, 512 devices: a whole 4x4x16 slice. The times are simulated.
512 devices in a mesh: ctx: 64 (over y, z_hi, x, core), head: 8 (over z_lo).
Axes of the slice: x: 4, y: 4, z: 16 (z_hi: 2, z_lo: 8; z = z_hi * 8 + z_lo), core: 2. Of those that a mesh axis runs over, the one named last changes fastest.
Arguments:
- query_raw: bfloat16 [16384, 5120], P('ctx', 'head'), may hold values from -9 to 9
- key_raw: bfloat16 [16384, 5120], P('ctx', 'head'), may hold values from -9 to 9
- values: bfloat16 [16384, 5120], P('ctx', 'head'), may hold values from -6 to 6
- out_grad: bfloat16 [16384, 5120], P('ctx', 'head'), may hold values from -128 to 128
- query_gain: float32 [5120], P('head'), may hold values from 0.25 to 1.75
- key_gain: float32 [5120], P('head'), may hold values from 0.25 to 1.75
- key_tiles: int32 [128, 4], P('ctx'), may hold values from 0 to 127, as said below
- global_ids: int32 [128], P('ctx'), may hold values from 0 to 16383, as said below
- readers: int32 [64, 64], P('ctx'), may hold values from 0 to 1, as said below
Outputs:
- query_grad: bfloat16 [16384, 5120], P('ctx', 'head')
- key_grad: bfloat16 [16384, 5120], P('ctx', 'head')
- value_grad: bfloat16 [16384, 5120], P('ctx', 'head')
Inputs may be any that keep to these rules, and one draw needn't show every extreme that they name: `key_tiles`: row t lists, ascending, the 4 tiles of 4 consecutive tile-frames of 1 tiles; every listed tile lies on an index of ctx at most 1 away from tile t's, and in every draw some tile reads a tile exactly 1 below and some tile one exactly 1 above. `global_ids`: entries c * 2 to (c + 1) * 2 - 1 are distinct ascending tokens of index c of ctx. `readers`: each row has either one 1 or all 64 entries 1; at least one row has all.
All inputs are finite; a program needn't handle non-finite values.
Results may differ from a plain program's by a relative error of at most 0.02.
Values may be sent and summed in bfloat16 or wider, within the bound.
A program may use at most 64 MiB of HBM per device.

v0:
```python
import jax
import jax.numpy as jnp
from jax import lax
from jax.sharding import PartitionSpec as P

HEAD_DIM = 128
D = 5120
TILE = 128
REACH = 1
G_DEV = 2
EPSILON = 1e-06


def passed_along(shard, axis, by):
    count = lax.axis_size(axis)
    return lax.ppermute(shard, axis, [(i, (i + by) % count) for i in range(count)])


def normalize(as_float, gain, squares):
    inverse = lax.rsqrt(squares[:, None] / D + EPSILON)
    return (inverse, (as_float * inverse * gain).astype(jnp.bfloat16))


def norm_grad(as_float, inverse, scaled, coeffs):
    return (inverse * scaled - as_float * inverse**3 * (coeffs[:, None] / D)).astype(jnp.bfloat16)


def body(
    query_raw, key_raw, values, out_grad, query_gain, key_gain, key_tiles, global_ids, readers
):
    tokens_here, width_here = query_raw.shape
    heads_here = width_here // HEAD_DIM
    tiles_here = tokens_here // TILE
    factor = HEAD_DIM ** (-0.5)
    device = lax.axis_index("ctx")
    query_rows = query_raw.astype(jnp.float32)
    key_rows = key_raw.astype(jnp.float32)
    query_sq, key_sq = lax.psum(
        (jnp.sum(query_rows * query_rows, axis=1), jnp.sum(key_rows * key_rows, axis=1)), "head"
    )
    query_inv, query_norm = normalize(query_rows, query_gain, query_sq)
    key_inv, key_norm = normalize(key_rows, key_gain, key_sq)
    own_rows = global_ids - device * tokens_here
    own_pair = jnp.stack([key_norm[own_rows], values[own_rows]])
    global_pair = lax.all_gather(own_pair, "ctx", axis=1, tiled=True)
    global_keys = global_pair[0].reshape(-1, heads_here, HEAD_DIM)
    global_vals = global_pair[1].reshape(-1, heads_here, HEAD_DIM)
    live_mask = jnp.repeat(readers[0] > 0, G_DEV)
    key_value = jnp.stack([key_norm, values])
    current = passed_along(key_value, "ctx", -REACH)
    pieces = [current]
    for hop_index in range(2 * REACH):
        current = passed_along(current, "ctx", 1)
        pieces.append(current)
    pieces = pieces[::-1]
    window_pair = jnp.concatenate(pieces, axis=1)
    first_tile = (device - REACH) * tiles_here
    local_tiles = key_tiles - first_tile
    window_rows = (
        local_tiles[:, :, None] * TILE + jnp.arange(TILE, dtype=jnp.int32)[None, None, :]
    ).reshape(tiles_here, -1)
    window_count = window_rows.shape[1]
    window_keys = window_pair[0][window_rows].reshape(
        tiles_here, window_count, heads_here, HEAD_DIM
    )
    window_vals = window_pair[1][window_rows].reshape(
        tiles_here, window_count, heads_here, HEAD_DIM
    )
    query_four = query_norm.reshape(tiles_here, TILE, heads_here, HEAD_DIM)
    grad_four = out_grad.reshape(tiles_here, TILE, heads_here, HEAD_DIM)

    def head_block(head_number):
        query_head = lax.dynamic_index_in_dim(query_four, head_number, 2, keepdims=False)
        grad_head = lax.dynamic_index_in_dim(grad_four, head_number, 2, keepdims=False)
        wkeys = lax.dynamic_index_in_dim(window_keys, head_number, 2, keepdims=False)
        wvals = lax.dynamic_index_in_dim(window_vals, head_number, 2, keepdims=False)
        gkeys = lax.dynamic_index_in_dim(global_keys, head_number, 1, keepdims=False)
        gvals = lax.dynamic_index_in_dim(global_vals, head_number, 1, keepdims=False)
        score_window = (
            jnp.einsum("tqd,tkd->tqk", query_head, wkeys, preferred_element_type=jnp.float32)
            * factor
        )
        score_global = (
            jnp.einsum("tqd,kd->tqk", query_head, gkeys, preferred_element_type=jnp.float32)
            * factor
        )
        score_global = jnp.where(live_mask, score_global, -jnp.inf)
        scores = jnp.concatenate([score_window, score_global], axis=2)
        largest = jnp.max(scores, axis=2, keepdims=True)
        log_total = largest + jnp.log(jnp.sum(jnp.exp(scores - largest), axis=2, keepdims=True))
        probs = jnp.exp(scores - log_total)
        probs_low = probs.astype(jnp.bfloat16)
        attended = jnp.einsum(
            "tqk,tkd->tqd", probs_low[..., :window_count], wvals, preferred_element_type=jnp.float32
        )
        attended = attended + jnp.einsum(
            "tqk,kd->tqd", probs_low[..., window_count:], gvals, preferred_element_type=jnp.float32
        )
        attended = lax.optimization_barrier(attended.astype(jnp.bfloat16))
        delta_rows = jnp.sum(grad_head.astype(jnp.float32) * attended.astype(jnp.float32), axis=2)
        dprob = jnp.concatenate(
            [
                jnp.einsum("tqd,tkd->tqk", grad_head, wvals, preferred_element_type=jnp.float32),
                jnp.einsum("tqd,kd->tqk", grad_head, gvals, preferred_element_type=jnp.float32),
            ],
            axis=2,
        )
        dscore = (probs * (dprob - delta_rows[..., None]) * factor).astype(jnp.bfloat16)
        grad_query = jnp.einsum(
            "tqk,tkd->tqd", dscore[..., :window_count], wkeys, preferred_element_type=jnp.float32
        )
        grad_query = grad_query + jnp.einsum(
            "tqk,kd->tqd", dscore[..., window_count:], gkeys, preferred_element_type=jnp.float32
        )
        window_dk = jnp.einsum(
            "tqk,tqd->tkd",
            dscore[..., :window_count],
            query_head,
            preferred_element_type=jnp.float32,
        )
        window_dv = jnp.einsum(
            "tqk,tqd->tkd",
            probs_low[..., :window_count],
            grad_head,
            preferred_element_type=jnp.float32,
        )
        global_dk = jnp.einsum(
            "tqk,tqd->kd",
            dscore[..., window_count:],
            query_head,
            preferred_element_type=jnp.float32,
        )
        global_dv = jnp.einsum(
            "tqk,tqd->kd",
            probs_low[..., window_count:],
            grad_head,
            preferred_element_type=jnp.float32,
        )
        return (grad_query, window_dk, window_dv, global_dk, global_dv)

    head_results = lax.map(head_block, jnp.arange(heads_here, dtype=jnp.int32))
    grad_query = jnp.moveaxis(head_results[0], 0, 2).reshape(tokens_here, width_here)
    window_dk = jnp.moveaxis(head_results[1], 0, 2).reshape(-1, width_here)
    window_dv = jnp.moveaxis(head_results[2], 0, 2).reshape(-1, width_here)
    global_dk = jnp.moveaxis(head_results[3], 0, 1).reshape(-1, width_here)
    global_dv = jnp.moveaxis(head_results[4], 0, 1).reshape(-1, width_here)
    window_grads = jnp.zeros((2, window_pair.shape[1], width_here), jnp.float32)
    window_grads = window_grads.at[:, window_rows.reshape(-1)].add(
        jnp.stack([window_dk, window_dv])
    )
    spread_grads = window_grads.reshape(2, 2 * REACH + 1, tokens_here, width_here)
    slots = [spread_grads[:, slot_index] for slot_index in range(2 * REACH + 1)]
    carried = slots[2 * REACH]
    for hop_index in range(2 * REACH):
        carried = (
            passed_along(carried.astype(jnp.bfloat16), "ctx", 1).astype(carried.dtype)
            + slots[2 * REACH - 1 - hop_index]
        )
    home_grads = passed_along(carried.astype(jnp.bfloat16), "ctx", -REACH).astype(carried.dtype)
    global_part = lax.psum_scatter(
        jnp.stack([global_dk, global_dv]), "ctx", scatter_dimension=1, tiled=True
    )
    home_grads = home_grads.at[:, own_rows].add(global_part)
    scaled_query = grad_query * query_gain
    scaled_key = home_grads[0] * key_gain
    query_dot, key_dot = lax.psum(
        (jnp.sum(scaled_query * query_rows, axis=1), jnp.sum(scaled_key * key_rows, axis=1)), "head"
    )
    query_grad = norm_grad(query_rows, query_inv, scaled_query, query_dot)
    key_grad = norm_grad(key_rows, key_inv, scaled_key, key_dot)
    return (query_grad, key_grad, home_grads[1].astype(jnp.bfloat16))


def solution(mesh):
    return jax.shard_map(
        body,
        mesh=mesh,
        in_specs=(
            P("ctx", "head"),
            P("ctx", "head"),
            P("ctx", "head"),
            P("ctx", "head"),
            P("head"),
            P("head"),
            P("ctx", None),
            P("ctx"),
            P("ctx", None),
        ),
        out_specs=(P("ctx", "head"), P("ctx", "head"), P("ctx", "head")),
        check_vma=False,
    )
```

profile of v0, /device:TPU:0, one launch (start us, length us, event | category | flops | bytes accessed | tf_op | source)
XLA Modules:
  0.0 1697.6 jit_solution(5765392369090235249)
XLA Ops:
  9.7 30.9 %all-reduce.2 = (f32[256]{0:T(256)S(1)}, f32[256]{0:T(256)S(1)}) all-reduce(f32[256]{0:T(256)S(1)} %fusion.68, f32[256]{0:T(256)S(1)} %fusion.75), channel_id=1, replica_groups=mesh['ctx'=64,'head'=8] {'head'}, use_global_device_ids=true, to_apply=%region_1.0 | all-reduce | flops 512 | bytes 4096 | tf_op jit(solution)/shard_map/psum | solution.py:38
  42.5 8.5 collective-permute-start
  53.0 8.4 collective-permute-done
  63.4 166.6 %all_gather.3 = bf16[2,128,640]{2,0,1:T(2,128)(2,1)S(1)} all-gather(bf16[2,2,640]{2,0,1:T(2,128)(2,1)S(1)} %copy.60), channel_id=1, replica_groups=mesh['ctx'=64,'head'=8] {'ctx'}, dimensions={1}, use_global_device_ids=true | all-gather | bytes 332800 | tf_op jit(solution)/shard_map/all_gather | solution.py:45
  233.7 2.4 collective-permute-start.2
  237.4 27.7 %collective-permute-done.2 = bf16[2,256,640]{2,1,0:T(8,128)(2,1)S(1)} collective-permute-done((bf16[2,256,640]{2,1,0:T(8,128)(2,1)S(1)}, bf16[2,256,640]{2,1,0:T(8,128)(2,1)S(1)}, u32[]{:S(2)}, u32[]{:S(2)}) %collective-permute-start.2) | collective-permute-done | bytes 655392 | tf_op jit(solution)/shard_map/ppermute | solution.py:16
  265.6 5.2 gather_fusion
  270.8 4.1 reshape.218
  276.7 5.2 gather_fusion.3
  281.9 4.1 reshape.220
  287.8 76.5 %while.19 = (s32[]{:T(128)}, f32[5,2,128,128]{3,2,1,0:T(8,128)}, f32[5,2,512,128]{3,2,1,0:T(8,128)}, f32[5,2,512,128]{3,2,1,0:T(8,128)}, f32[5,128,128]{1,2,0:T(...) while((s32[]{:T(128)}, f32[5,2,128,128]{3,2,1,0:T(8,128)}, ...), condition=%wide.region_9.10_spmd.clone, body=%wide.region_4.9_spmd.clone.sunk | while | flops 254377472 | bytes 9916299 | solution.py:141
  364.3 5.1 copy.72
  369.3 3.7 stack_reshape.12
  373.0 5.1 copy.73
  378.1 4.8 stack_reshape.13
  383.0 4.7 maximum_bitcast_fusion
  387.7 8.8 copy.74
  396.5 3.0 broadcast_in_dim.59
  399.4 131.0 %scatter_fusion = f32[2,768,640]{2,0,1:T(2,128)} fusion(f32[2,768,640]{2,0,1:T(2,128)} %broadcast_in_dim.59, s32[1024]{0:T(1024)S(1)} %bitcast.214, f32[1024,2,640]{2,1,0:T(2,128)} %copy.74), kind=kCustom, calls=%fused_computation.4 | custom fusion | flops 1310720 | bytes 15732736 | tf_op jit(solution)/shard_map/scatter-add | solution.py:148
  534.2 24.1 %collective-permute-done.3 = bf16[2,256,640]{2,0,1:T(2,128)(2,1)S(1)} collective-permute-done((bf16[2,256,640]{2,0,1:T(2,128)(2,1)S(1)}, bf16[2,256,640]{2,0,1:T(2,128)(2,1)S(1)}, u32[]{:S(2)}, u32[]{:S(2)}) %collective-permute-start.3) | collective-permute-done | bytes 655392 | tf_op jit(solution)/shard_map/ppermute | solution.py:16
  560.3 2.1 collective-permute-start.4
  564.8 20.6 %collective-permute-done.4 = bf16[2,256,640]{2,0,1:T(2,128)(2,1)S(1)} collective-permute-done((bf16[2,256,640]{2,0,1:T(2,128)(2,1)S(1)}, bf16[2,256,640]{2,0,1:T(2,128)(2,1)S(1)}, u32[]{:S(2)}, u32[]{:S(2)}) %collective-permute-start.4) | collective-permute-done | bytes 655392 | tf_op jit(solution)/shard_map/ppermute | solution.py:16
  592.3 1057.7 %all-reduce.5.cloned.1.call-done = f32[2,128,640]{2,0,1:T(2,128)} async-done(((f32[2,128,640]{2,0,1:T(2,128)}), f32[2,128,640]{2,0,1:T(2,128)}) %all-reduce.5.cloned.1.call-update) | async-done | bytes 655376
  1655.1 32.8 %all-reduce.1 = (f32[256]{0:T(256)S(1)}, f32[256]{0:T(256)S(1)}) all-reduce(f32[256]{0:T(256)S(1)} %fusion.74, f32[256]{0:T(256)S(1)} %fusion.81), channel_id=1, replica_groups=mesh['ctx'=64,'head'=8] {'head'}, use_global_device_ids=true, to_apply=%region_11.12 | all-reduce | flops 512 | bytes 4096 | tf_op jit(solution)/shard_map/psum | solution.py:166
  (251 shorter events, 104.9 us)
Async XLA Ops:
  7.2 45.1 %copy-start = (bf16[256,640]{1,0:T(8,128)(2,1)S(1)}, bf16[256,640]{1,0:T(8,128)(2,1)}, u32[]{:S(2)}) copy-start(bf16[256,640]{1,0:T(8,128)(2,1)} %param.12) | copy-start | bytes 983044
  7.2 45.1 %copy-start.9 = (f32[640]{0:T(1024)S(1)}, f32[640]{0:T(1024)}, u32[]{:S(2)}) copy-start(f32[640]{0:T(1024)} %param.16) | copy-start | bytes 7684
  7.2 35.2 %copy-start.6 = (bf16[256,640]{1,0:T(8,128)(2,1)S(1)}, bf16[256,640]{1,0:T(8,128)(2,1)}, u32[]{:S(2)}) copy-start(bf16[256,640]{1,0:T(8,128)(2,1)} %param.13) | copy-start | bytes 983044
  7.2 43.9 %copy-start.21 = (s32[2,4]{1,0:T(2,128)S(1)}, s32[2,4]{1,0:T(2,128)}, u32[]{:S(2)}) copy-start(s32[2,4]{1,0:T(2,128)} %param.17) | copy-start | bytes 100
  7.2 44.0 %copy-start.22 = (s32[2]{0:T(128)S(1)}, s32[2]{0:T(128)}, u32[]{:S(2)}) copy-start(s32[2]{0:T(128)} %param.18) | copy-start | bytes 28
  7.2 1642.8 %all-reduce.5.cloned.1.call-start = ((), (), s32[]{:S(2)}) async-start(), calls=%async_computation | async-start | bytes 1310720
  8.5 223.8 %copy-start.2 = (bf16[256,640]{0,1:T(8,128)(2,1)}, bf16[256,640]{0,1:T(8,128)(2,1)S(1)}, u32[]{:S(2)}) copy-start(bf16[256,640]{0,1:T(8,128)(2,1)S(1)} %copy.58) | copy-start | bytes 983044
  41.2 191.0 %copy-start.15 = (f32[256]{0:T(256)}, f32[256]{0:T(256)S(1)}, u32[]{:S(2)}) copy-start(f32[256]{0:T(256)S(1)} %get-tuple-element.207) | copy-start | bytes 3076
  42.5 189.8 %copy-start.10 = (f32[640]{0:T(1024)S(1)}, f32[640]{0:T(1024)}, u32[]{:S(2)}) copy-start(f32[640]{0:T(1024)} %param.15) | copy-start | bytes 7684
  42.5 18.9 %collective-permute-start = (bf16[2,256,640]{2,1,0:T(8,128)(2,1)S(1)}, bf16[2,256,640]{2,1,0:T(8,128)(2,1)S(1)}, u32[]{:S(2)}, u32[]{:S(2)}) collective-permute-start(bf16[2,256,640]{2,1,0:T(8,128)(2,1)S(1)} %pad_maximum_fusion.1), channel_id=1, source_target_pairs={{0,504},{8,0},{16,8},{24,16},{32,24},{40,32},{48,40},{56,48},{64,5... | collective-permute-start | bytes 1966088 | tf_op jit(solution)/shard_map/ppermute | solution.py:16
  61.4 172.3 %collective-permute-start.1 = (bf16[2,256,640]{2,1,0:T(8,128)(2,1)S(1)}, bf16[2,256,640]{2,1,0:T(8,128)(2,1)S(1)}, u32[]{:S(2)}, u32[]{:S(2)}) collective-permute-start(bf16[2,256,640]{2,1,0:T(8,128)(2,1)S(1)} %collective-permute-done), channel_id=1, source_target_pairs={{0,8},{8,16},{16,24},{24,32},{32,40},{40,48},{48,56},{56,64},{64,7... | collective-permute-start | bytes 1966088 | tf_op jit(solution)/shard_map/ppermute | solution.py:16
  63.4 169.9 %copy-start.8 = (bf16[256,640]{1,0:T(8,128)(2,1)S(1)}, bf16[256,640]{1,0:T(8,128)(2,1)}, u32[]{:S(2)}) copy-start(bf16[256,640]{1,0:T(8,128)(2,1)} %param.14) | copy-start | bytes 983044
  233.7 31.4 %collective-permute-start.2 = (bf16[2,256,640]{2,1,0:T(8,128)(2,1)S(1)}, bf16[2,256,640]{2,1,0:T(8,128)(2,1)S(1)}, u32[]{:S(2)}, u32[]{:S(2)}) collective-permute-start(bf16[2,256,640]{2,1,0:T(8,128)(2,1)S(1)} %collective-permute-done.1), channel_id=1, source_target_pairs={{0,8},{8,16},{16,24},{24,32},{32,40},{40,48},{48,56},{56,64},{64,7... | collective-permute-start | bytes 1966088 | tf_op jit(solution)/shard_map/ppermute | solution.py:16
  530.4 32.0 %copy-start.7 = (f32[5,128,128]{1,2,0:T(8,128)S(1)}, f32[5,128,128]{1,2,0:T(8,128)}, u32[]{:S(2)}) copy-start(f32[5,128,128]{1,2,0:T(8,128)} %get-tuple-element.82) | copy-start | bytes 983044
  532.3 26.0 %collective-permute-start.3 = (bf16[2,256,640]{2,0,1:T(2,128)(2,1)S(1)}, bf16[2,256,640]{2,0,1:T(2,128)(2,1)S(1)}, u32[]{:S(2)}, u32[]{:S(2)}) collective-permute-start(bf16[2,256,640]{2,0,1:T(2,128)(2,1)S(1)} %fusion.82), channel_id=1, source_target_pairs={{0,8},{8,16},{16,24},{24,32},{32,40},{40,48},{48,56},{56,64},{64,7... | collective-permute-start | bytes 1966088 | tf_op jit(solution)/shard_map/ppermute | solution.py:16
  560.3 25.0 %collective-permute-start.4 = (bf16[2,256,640]{2,0,1:T(2,128)(2,1)S(1)}, bf16[2,256,640]{2,0,1:T(2,128)(2,1)S(1)}, u32[]{:S(2)}, u32[]{:S(2)}) collective-permute-start(bf16[2,256,640]{2,0,1:T(2,128)(2,1)S(1)} %fusion.67), channel_id=1, source_target_pairs={{0,8},{8,16},{16,24},{24,32},{32,40},{40,48},{48,56},{56,64},{64,7... | collective-permute-start | bytes 1966088 | tf_op jit(solution)/shard_map/ppermute | solution.py:16
  564.8 27.4 %copy-start.3 = (bf16[256,640]{0,1:T(8,128)(2,1)S(1)}, bf16[256,640]{0,1:T(8,128)(2,1)}, u32[]{:S(2)}) copy-start(bf16[256,640]{0,1:T(8,128)(2,1)} %copy-done.2) | copy-start | bytes 983044
  587.4 1063.4 %collective-permute-start.5 = (bf16[2,256,640]{2,0,1:T(2,128)(2,1)S(1)}, bf16[2,256,640]{2,0,1:T(2,128)(2,1)}, u32[]{:S(2)}, u32[]{:S(2)}) collective-permute-start(bf16[2,256,640]{2,0,1:T(2,128)(2,1)S(1)} %fusion.65), channel_id=1, source_target_pairs={{0,504},{8,0},{16,8},{24,16},{32,24},{40,32},{48,40},{56,48},{64,5... | collective-permute-start | bytes 1966088 | tf_op jit(solution)/shard_map/ppermute | solution.py:16
  591.2 1061.1 %copy-start.20 = (s32[2]{0:T(128)S(1)}, s32[2]{0:T(128)}, u32[]{:S(2)}) copy-start(s32[2]{0:T(128)} %copy-done.19) | copy-start | bytes 28
  1652.3 35.7 %copy-start.16 = (f32[256]{0:T(256)S(1)}, f32[256]{0:T(256)}, u32[]{:S(2)}) copy-start(f32[256]{0:T(256)} %copy-done.15) | copy-start | bytes 3076
  1652.3 35.7 %copy-start.18 = (f32[256]{0:T(256)S(1)}, f32[256]{0:T(256)}, u32[]{:S(2)}) copy-start(f32[256]{0:T(256)} %get-tuple-element.208) | copy-start | bytes 3076
  1655.0 34.1 %copy-start.4 = (bf16[1,256,640]{2,0,1:T(2,128)(2,1)S(1)}, bf16[1,256,640]{2,0,1:T(2,128)(2,1)}, u32[]{:S(2)}) copy-start(bf16[1,256,640]{2,0,1:T(2,128)(2,1)} %slice.111) | copy-start | bytes 983044
  1655.0 34.9 %copy-start.14 = (f32[256]{0:T(256)S(1)}, f32[256]{0:T(256)}, u32[]{:S(2)}) copy-start(f32[256]{0:T(256)} %copy-done.13) | copy-start | bytes 3076
  1655.0 34.9 %copy-start.17 = (f32[256]{0:T(256)S(1)}, f32[256]{0:T(256)}, u32[]{:S(2)}) copy-start(f32[256]{0:T(256)} %get-tuple-element.203) | copy-start | bytes 3076
  (17 other events, 137.7 us)
Sparse Core Ops, SparseCore 0:
  564.9 1085.0 all-reduce.4
where the time goes:
time: 1700 us
  waiting for transfers between devices  1140 us (67%)
  blocking collectives  230 us (14%)
  other arithmetic  153 us (9%)
  local copies, waits for them, and re-layouts  84.9 us (5%)
  matrix products  46.1 us (3%)
  starting transfers between devices  18.9 us (1%)
    unnamed x2, waiting for transfers between devices  1060 us
    all_gather x1, blocking collectives, body(): global_pair = lax.all_gather(own_pair, 'ctx', axis=1, tiled=True)  167 us
    scatter-add x1, other arithmetic, body(): window_grads.at[:, window_rows.reshape(-1)]  131 us
    ppermute x6, waiting for transfers between devices, passed_along(): lax.ppermute(shard, axis, [(i, (i + by) % count) for i in range(count)])  80.8 us
  transfers between devices with their start and end apart: 7, of which 5 were waited for; matrix products, arithmetic and copies ran while one was open for 1% of the time, Pallas kernels for 0%

commit v1 on v0

--- a/solution.py
+++ b/solution.py
@@ -42,7 +42,9 @@
     key_inv, key_norm = normalize(key_rows, key_gain, key_sq)
     own_rows = global_ids - device * tokens_here
     own_pair = jnp.stack([key_norm[own_rows], values[own_rows]])
-    global_pair = lax.all_gather(own_pair, "ctx", axis=1, tiled=True)
+    global_pair = jnp.concatenate(
+        lax.all_to_all(jnp.stack([own_pair] * lax.axis_size("ctx")), "ctx", 0, 0), axis=1
+    )
     global_keys = global_pair[0].reshape(-1, heads_here, HEAD_DIM)
     global_vals = global_pair[1].reshape(-1, heads_here, HEAD_DIM)
     live_mask = jnp.repeat(readers[0] > 0, G_DEV)

time: 1700 us -> 1580 us (0.929)
  blocking collectives: 230 us -> 63.8 us
  waiting for transfers between devices: 1140 us -> 1170 us
    all_gather x1 -> x0, blocking collectives: 167 us -> none  [body(): global_pair = lax.all_gather(own_pair, 'ctx', axis=1, tiled=True)]
    ppermute x6, waiting for transfers between devices: 80.8 us -> 113 us  [passed_along(): lax.ppermute(shard, axis, [(i, (i + by) % count) for i in range(count)])]
  transfers between devices with their start and end apart: 7 -> 8, of which waited for: 5 -> 6; matrix products, arithmetic and copies ran while one was open for 1% -> 1% of each run, Pallas kernels for 0% -> 0%
where the time goes in v1:
time: 1580 us; the launch traced here: 1570 us
  waiting for transfers between devices  1170 us (74%)
  other arithmetic  153 us (10%)
  local copies, waits for them, and re-layouts  85.4 us (5%)
  blocking collectives  63.8 us (4%)
  matrix products  46.2 us (3%)
  starting transfers between devices  25.7 us (2%)
    unnamed x2, waiting for transfers between devices  1060 us
    scatter-add x1, other arithmetic, body(): window_grads.at[:, window_rows.reshape(-1)]  131 us
    ppermute x6, waiting for transfers between devices, passed_along(): lax.ppermute(shard, axis, [(i, (i + by) % count) for i in range(count)])  113 us
    psum x1, blocking collectives, body(): lax.psum((jnp.sum(scaled_query * query_rows, axis=1), jnp.sum(scaled_key...  32.8 us
  transfers between devices with their start and end apart: 8, of which 6 were waited for; matrix products, arithmetic and copies ran while one was open for 1% of the time, Pallas kernels for 0%

profile of v1, /device:TPU:0, one launch (start us, length us, event | category | flops | bytes accessed | tf_op | source)
XLA Modules:
  0.0 1570.4 jit_solution(3217866990400071710)
XLA Ops:
  9.7 30.9 %all-reduce.2 = (f32[256]{0:T(256)S(1)}, f32[256]{0:T(256)S(1)}) all-reduce(f32[256]{0:T(256)S(1)} %fusion.68, f32[256]{0:T(256)S(1)} %fusion.75), channel_id=1, replica_groups=mesh['ctx'=64,'head'=8] {'head'}, use_global_device_ids=true, to_apply=%region_1.0 | all-reduce | flops 512 | bytes 4096 | tf_op jit(solution)/shard_map/psum | solution.py:38
  42.5 8.5 collective-permute-start
  54.0 7.2 all-to-all-start
  61.3 3.5 collective-permute-done
  68.3 32.5 %collective-permute-done.1 = bf16[2,256,640]{2,1,0:T(8,128)(2,1)S(1)} collective-permute-done((bf16[2,256,640]{2,1,0:T(8,128)(2,1)S(1)}, bf16[2,256,640]{2,1,0:T(8,128)(2,1)S(1)}, u32[]{:S(2)}, u32[]{:S(2)}) %collective-permute-start.1) | collective-permute-done | bytes 655392 | tf_op jit(solution)/shard_map/ppermute | solution.py:16
  105.9 28.8 %collective-permute-done.2 = bf16[2,256,640]{2,1,0:T(8,128)(2,1)S(1)} collective-permute-done((bf16[2,256,640]{2,1,0:T(8,128)(2,1)S(1)}, bf16[2,256,640]{2,1,0:T(8,128)(2,1)S(1)}, u32[]{:S(2)}, u32[]{:S(2)}) %collective-permute-start.2) | collective-permute-done | bytes 655392 | tf_op jit(solution)/shard_map/ppermute | solution.py:16
  135.2 5.2 gather_fusion
  140.4 4.1 reshape.229
  146.3 5.2 gather_fusion.3
  151.5 4.1 reshape.231
  157.4 76.4 %while.19 = (s32[]{:T(128)}, f32[5,2,128,128]{3,2,1,0:T(8,128)}, f32[5,2,512,128]{3,2,1,0:T(8,128)}, f32[5,2,512,128]{3,2,1,0:T(8,128)}, f32[5,128,128]{1,2,0:T(...) while((s32[]{:T(128)}, f32[5,2,128,128]{3,2,1,0:T(8,128)}, ...), condition=%wide.region_9.10_spmd.clone, body=%wide.region_4.9_spmd.clone.sunk | while | flops 254377472 | bytes 9916299 | solution.py:143
  233.8 5.1 copy.65
  238.9 3.7 stack_reshape.12
  242.6 5.1 copy.66
  247.7 4.8 stack_reshape.13
  252.5 4.7 maximum_bitcast_fusion
  257.2 8.8 copy.67
  266.0 2.9 broadcast_in_dim.59
  269.0 130.9 %scatter_fusion = f32[2,768,640]{2,0,1:T(2,128)} fusion(f32[2,768,640]{2,0,1:T(2,128)} %broadcast_in_dim.59, s32[1024]{0:T(1024)S(1)} %bitcast.212, f32[1024,2,640]{2,1,0:T(2,128)} %copy.67), kind=kCustom, calls=%fused_computation.4 | custom fusion | flops 1310720 | bytes 15732736 | tf_op jit(solution)/shard_map/scatter-add | solution.py:150
  401.7 2.1 collective-permute-start.3
  403.8 22.7 %collective-permute-done.3 = bf16[2,256,640]{2,0,1:T(2,128)(2,1)S(1)} collective-permute-done((bf16[2,256,640]{2,0,1:T(2,128)(2,1)S(1)}, bf16[2,256,640]{2,0,1:T(2,128)(2,1)S(1)}, u32[]{:S(2)}, u32[]{:S(2)}) %collective-permute-start.3) | collective-permute-done | bytes 655392 | tf_op jit(solution)/shard_map/ppermute | solution.py:16
  432.8 25.8 %collective-permute-done.4 = bf16[2,256,640]{2,0,1:T(2,128)(2,1)S(1)} collective-permute-done((bf16[2,256,640]{2,0,1:T(2,128)(2,1)S(1)}, bf16[2,256,640]{2,0,1:T(2,128)(2,1)S(1)}, u32[]{:S(2)}, u32[]{:S(2)}) %collective-permute-start.4) | collective-permute-done | bytes 655392 | tf_op jit(solution)/shard_map/ppermute | solution.py:16
  465.5 1057.3 %all-reduce.5.cloned.1.call-done = f32[2,128,640]{2,0,1:T(2,128)} async-done(((f32[2,128,640]{2,0,1:T(2,128)}), f32[2,128,640]{2,0,1:T(2,128)}) %all-reduce.5.cloned.1.call-update) | async-done | bytes 655376
  1527.9 32.8 %all-reduce.1 = (f32[256]{0:T(256)S(1)}, f32[256]{0:T(256)S(1)}) all-reduce(f32[256]{0:T(256)S(1)} %fusion.74, f32[256]{0:T(256)S(1)} %fusion.81), channel_id=1, replica_groups=mesh['ctx'=64,'head'=8] {'head'}, use_global_device_ids=true, to_apply=%region_11.12 | all-reduce | flops 512 | bytes 4096 | tf_op jit(solution)/shard_map/psum | solution.py:168
  (254 shorter events, 107.6 us)
Async XLA Ops:
  7.2 45.2 %copy-start = (bf16[256,640]{1,0:T(8,128)(2,1)S(1)}, bf16[256,640]{1,0:T(8,128)(2,1)}, u32[]{:S(2)}) copy-start(bf16[256,640]{1,0:T(8,128)(2,1)} %param.12) | copy-start | bytes 983044
  7.2 45.2 %copy-start.9 = (f32[640]{0:T(1024)S(1)}, f32[640]{0:T(1024)}, u32[]{:S(2)}) copy-start(f32[640]{0:T(1024)} %param.16) | copy-start | bytes 7684
  7.2 35.2 %copy-start.6 = (bf16[256,640]{1,0:T(8,128)(2,1)S(1)}, bf16[256,640]{1,0:T(8,128)(2,1)}, u32[]{:S(2)}) copy-start(bf16[256,640]{1,0:T(8,128)(2,1)} %param.13) | copy-start | bytes 983044
  7.2 43.8 %copy-start.21 = (s32[2,4]{1,0:T(2,128)S(1)}, s32[2,4]{1,0:T(2,128)}, u32[]{:S(2)}) copy-start(s32[2,4]{1,0:T(2,128)} %param.17) | copy-start | bytes 100
  7.2 43.9 %copy-start.22 = (s32[2]{0:T(128)S(1)}, s32[2]{0:T(128)}, u32[]{:S(2)}) copy-start(s32[2]{0:T(128)} %param.18) | copy-start | bytes 28
  8.4 58.3 %copy-start.2 = (bf16[256,640]{0,1:T(8,128)(2,1)}, bf16[256,640]{0,1:T(8,128)(2,1)S(1)}, u32[]{:S(2)}) copy-start(bf16[256,640]{0,1:T(8,128)(2,1)S(1)} %copy.54) | copy-start | bytes 983044
  9.7 57.1 %copy-start.10 = (f32[640]{0:T(1024)S(1)}, f32[640]{0:T(1024)}, u32[]{:S(2)}) copy-start(f32[640]{0:T(1024)} %param.15) | copy-start | bytes 7684
  42.5 22.3 %collective-permute-start = (bf16[2,256,640]{2,1,0:T(8,128)(2,1)S(1)}, bf16[2,256,640]{2,1,0:T(8,128)(2,1)S(1)}, u32[]{:S(2)}, u32[]{:S(2)}) collective-permute-start(bf16[2,256,640]{2,1,0:T(8,128)(2,1)S(1)} %pad_maximum_fusion.1), channel_id=1, source_target_pairs={{0,504},{8,0},{16,8},{24,16},{32,24},{40,32},{48,40},{56,48},{64,5... | collective-permute-start | bytes 1966088 | tf_op jit(solution)/shard_map/ppermute | solution.py:16
  53.1 49.8 %copy-start.23 = (s32[1,64]{1,0:T(1,128)S(1)}, s32[1,64]{1,0:T(1,128)}, u32[]{:S(2)}) copy-start(s32[1,64]{1,0:T(1,128)} %param.19) | copy-start | bytes 772
  54.0 50.0 %all-to-all-start = ((bf16[64,2,2,640]{3,2,1,0:T(2,128)(2,1)}), bf16[64,2,2,640]{3,2,1,0:T(2,128)(2,1)S(1)}, u32[]{:S(2)}, u32[]{:S(2)}) async-start(bf16[64,2,2,640]{3,2,1,0:T(2,128)(2,1)} %stack.24), calls=%async_computation | async-start | bytes 655360 | tf_op jit(solution)/shard_map/all_to_all | solution.py:46
  61.2 1461.6 %all-reduce.5.cloned.1.call-start = ((), (), s32[]{:S(2)}) async-start(), calls=%async_computation.1 | async-start | bytes 1310720
  64.8 36.0 %collective-permute-start.1 = (bf16[2,256,640]{2,1,0:T(8,128)(2,1)S(1)}, bf16[2,256,640]{2,1,0:T(8,128)(2,1)S(1)}, u32[]{:S(2)}, u32[]{:S(2)}) collective-permute-start(bf16[2,256,640]{2,1,0:T(8,128)(2,1)S(1)} %collective-permute-done), channel_id=1, source_target_pairs={{0,8},{8,16},{16,24},{24,32},{32,40},{40,48},{48,56},{56,64},{64,7... | collective-permute-start | bytes 1966088 | tf_op jit(solution)/shard_map/ppermute | solution.py:16
  100.8 34.0 %collective-permute-start.2 = (bf16[2,256,640]{2,1,0:T(8,128)(2,1)S(1)}, bf16[2,256,640]{2,1,0:T(8,128)(2,1)S(1)}, u32[]{:S(2)}, u32[]{:S(2)}) collective-permute-start(bf16[2,256,640]{2,1,0:T(8,128)(2,1)S(1)} %collective-permute-done.1), channel_id=1, source_target_pairs={{0,8},{8,16},{16,24},{24,32},{32,40},{40,48},{48,56},{56,64},{64,7... | collective-permute-start | bytes 1966088 | tf_op jit(solution)/shard_map/ppermute | solution.py:16
  401.7 24.8 %collective-permute-start.3 = (bf16[2,256,640]{2,0,1:T(2,128)(2,1)S(1)}, bf16[2,256,640]{2,0,1:T(2,128)(2,1)S(1)}, u32[]{:S(2)}, u32[]{:S(2)}) collective-permute-start(bf16[2,256,640]{2,0,1:T(2,128)(2,1)S(1)} %fusion.82), channel_id=1, source_target_pairs={{0,8},{8,16},{16,24},{24,32},{32,40},{40,48},{48,56},{56,64},{64,7... | collective-permute-start | bytes 1966088 | tf_op jit(solution)/shard_map/ppermute | solution.py:16
  428.6 30.0 %collective-permute-start.4 = (bf16[2,256,640]{2,0,1:T(2,128)(2,1)S(1)}, bf16[2,256,640]{2,0,1:T(2,128)(2,1)S(1)}, u32[]{:S(2)}, u32[]{:S(2)}) collective-permute-start(bf16[2,256,640]{2,0,1:T(2,128)(2,1)S(1)} %fusion.67), channel_id=1, source_target_pairs={{0,8},{8,16},{16,24},{24,32},{32,40},{40,48},{48,56},{56,64},{64,7... | collective-permute-start | bytes 1966088 | tf_op jit(solution)/shard_map/ppermute | solution.py:16
  432.8 32.6 %copy-start.3 = (bf16[256,640]{0,1:T(8,128)(2,1)S(1)}, bf16[256,640]{0,1:T(8,128)(2,1)}, u32[]{:S(2)}) copy-start(bf16[256,640]{0,1:T(8,128)(2,1)} %copy-done.2) | copy-start | bytes 983044
  432.8 32.6 %copy-start.11 = (f32[640]{0:T(1024)S(1)}, f32[640]{0:T(1024)}, u32[]{:S(2)}) copy-start(f32[640]{0:T(1024)} %param.15) | copy-start | bytes 7684
  460.6 1063.0 %collective-permute-start.5 = (bf16[2,256,640]{2,0,1:T(2,128)(2,1)S(1)}, bf16[2,256,640]{2,0,1:T(2,128)(2,1)}, u32[]{:S(2)}, u32[]{:S(2)}) collective-permute-start(bf16[2,256,640]{2,0,1:T(2,128)(2,1)S(1)} %fusion.65), channel_id=1, source_target_pairs={{0,504},{8,0},{16,8},{24,16},{32,24},{40,32},{48,40},{56,48},{64,5... | collective-permute-start | bytes 1966088 | tf_op jit(solution)/shard_map/ppermute | solution.py:16
  464.4 1060.7 %copy-start.20 = (s32[2]{0:T(128)S(1)}, s32[2]{0:T(128)}, u32[]{:S(2)}) copy-start(s32[2]{0:T(128)} %copy-done.19) | copy-start | bytes 28
  1525.1 35.7 %copy-start.16 = (f32[256]{0:T(256)S(1)}, f32[256]{0:T(256)}, u32[]{:S(2)}) copy-start(f32[256]{0:T(256)} %copy-done.15) | copy-start | bytes 3076
  1525.1 35.7 %copy-start.18 = (f32[256]{0:T(256)S(1)}, f32[256]{0:T(256)}, u32[]{:S(2)}) copy-start(f32[256]{0:T(256)} %get-tuple-element.208) | copy-start | bytes 3076
  1527.7 34.1 %copy-start.4 = (bf16[1,256,640]{2,0,1:T(2,128)(2,1)S(1)}, bf16[1,256,640]{2,0,1:T(2,128)(2,1)}, u32[]{:S(2)}) copy-start(bf16[1,256,640]{2,0,1:T(2,128)(2,1)} %slice.113) | copy-start | bytes 983044
  1527.7 34.9 %copy-start.14 = (f32[256]{0:T(256)S(1)}, f32[256]{0:T(256)}, u32[]{:S(2)}) copy-start(f32[256]{0:T(256)} %copy-done.13) | copy-start | bytes 3076
  1527.7 34.9 %copy-start.17 = (f32[256]{0:T(256)S(1)}, f32[256]{0:T(256)}, u32[]{:S(2)}) copy-start(f32[256]{0:T(256)} %get-tuple-element.203) | copy-start | bytes 3076
  (18 other events, 181.4 us)
Sparse Core Ops, SparseCore 0:
  432.9 1089.8 all-reduce.4
